TPU v7x, 32 devices: a whole 2x2x4 slice. The times are simulated.
32 devices in a mesh: layer: 2 (over core), row: 1, col: 16 (over z, y, x).
Axes of the slice: x: 2, y: 2, z: 4, core: 2. Of those that a mesh axis runs over, the one named last changes fastest.
Arguments:
- x_blocks: bfloat16 [1, 16, 32, 128, 128], P('row', 'col', 'layer'), may hold values from -0.5 to 0.5
- h_blocks: bfloat16 [1, 16, 32, 128, 128], P('row', 'col', 'layer'), may hold values from -1.5 to 1.5
- a_src: int32 [1, 16, 2, 128, 8], P('row', 'col', 'layer'), may hold values from 0 to 15, all different within a row; in each aligned block of 128 rows (0 to 127, 128 to 255, ..., all dimensions but the last counted through in order) at most 96 rows name the same one
- a_off: int32 [1, 16, 2, 128, 8], P('row', 'col', 'layer'), may hold values from 0 to 15
- b_slot: int32 [1, 16, 2, 128, 8], P('row', 'col', 'layer'), may hold values from 0 to 15
Outputs:
- product_blocks: bfloat16 [1, 16, 128, 128, 128], P('row', 'col', 'layer')
Inputs may be any that keep to these rules, and one draw needn't show every extreme that they name: `a_src`: the 8 sources of one product block are different; among the rows of one device (one owner and group) no column owner is named by more than 96 contributions, a bound that some block reaches. `b_slot`: index into the column panel of 16 blocks.
All inputs are finite; a program needn't handle non-finite values.
Results may differ from a plain program's by a relative error of at most 0.0051.
Values may be sent and summed in bfloat16 or wider, within the bound.
A program may use at most 192 MiB of HBM per device.

v0:
```python
import jax
import jax.numpy as jnp
from jax import lax
from jax.sharding import PartitionSpec as P


def block_terms(row_panel, col_panel, left_list, b_list):
    total = jnp.zeros((left_list.shape[0], col_panel.shape[1], col_panel.shape[2]), jnp.float32)
    for term in range(left_list.shape[1]):
        total = total + jnp.einsum(
            "pij,pjk->pik",
            row_panel[left_list[:, term]],
            col_panel[b_list[:, term]],
            preferred_element_type=jnp.float32,
        )
    return total


def on_device(x_blocks, h_blocks, a_src, a_off, b_slot):
    x_local = x_blocks[0, 0]
    h_local = h_blocks[0, 0]
    src_list = a_src[0, 0, 0]
    off_list = a_off[0, 0, 0]
    b_list = b_slot[0, 0, 0]
    shard_blocks = x_local.shape[0]
    owned_rows = src_list.shape[0]
    col_panel = lax.all_gather(h_local, "row", axis=0, tiled=True)
    row_panel = lax.all_gather(x_local, "col", axis=0, tiled=True)
    select = jnp.arange(owned_rows, dtype=jnp.int32)
    left_list = src_list[select] * shard_blocks + off_list[select]
    partial_value = (
        block_terms(row_panel, col_panel, left_list, b_list[select])
        .astype(jnp.bfloat16)
        .astype(jnp.float32)
    )
    summed = lax.psum_scatter(
        partial_value.astype(jnp.bfloat16), "layer", scatter_dimension=0, tiled=True
    )
    return summed[None, None]


def solution(mesh):
    placed = (
        P("row", "col", "layer", None, None),
        P("row", "col", "layer", None, None),
        P("row", "col", "layer", None, None),
        P("row", "col", "layer", None, None),
        P("row", "col", "layer", None, None),
    )
    return jax.shard_map(
        on_device,
        mesh=mesh,
        in_specs=placed,
        out_specs=P("row", "col", "layer", None, None),
        check_vma=False,
    )
```

profile of v0, /device:TPU:0, one launch (start us, length us, event | category | flops | bytes accessed | tf_op | source)
XLA Modules:
  0.0 261.0 jit_solution(2108247169165780425)
XLA Ops:
  6.5 0.0 copy-start
  6.5 0.0 all-gather.3.cloned.1.call-start
  6.5 0.7 all-gather.3.cloned.1.call-update
  7.3 0.0 reduce-scatter.2.cloned.1.call-start
  7.3 0.8 copy.13
  8.1 0.8 copy.14
  8.9 0.6 gather_fusion
  9.5 0.6 gather_fusion.1
  10.2 0.8 copy.15
  11.0 0.6 gather_fusion.3
  11.6 0.4 fusion.15
  12.0 0.0 copy-done
  12.0 3.0 %gather_fusion.6 = bf16[128,128,128]{2,1,0:T(8,128)(2,1)} fusion(bf16[16,128,128]{2,1,0:T(8,128)(2,1)S(1)} %bitcast.24, s32[1024]{0:T(1024)S(1)} %get-tuple-element.35), kind=kCustom, calls=%fused_computation.6 | custom fusion | bytes 8389120 | tf_op jit(solution)/shard_map/gather | solution.py:13
  15.0 3.0 %gather_fusion.10 = bf16[128,128,128]{2,1,0:T(8,128)(2,1)} fusion(bf16[16,128,128]{2,1,0:T(8,128)(2,1)S(1)} %bitcast.26, s32[1024]{0:T(1024)S(1)} %get-tuple-element.33), kind=kCustom, calls=%fused_computation.10 | custom fusion | bytes 8389120 | tf_op jit(solution)/shard_map/gather | solution.py:13
  18.1 3.0 %gather_fusion.14 = bf16[128,128,128]{2,1,0:T(8,128)(2,1)} fusion(bf16[16,128,128]{2,1,0:T(8,128)(2,1)S(1)} %bitcast.28, s32[1024]{0:T(1024)S(1)} %get-tuple-element.31), kind=kCustom, calls=%fused_computation.14 | custom fusion | bytes 8389120 | tf_op jit(solution)/shard_map/gather | solution.py:13
  21.1 3.0 %gather_fusion.18 = bf16[128,128,128]{2,1,0:T(8,128)(2,1)} fusion(bf16[16,128,128]{2,1,0:T(8,128)(2,1)S(1)} %bitcast.30, s32[1024]{0:T(1024)S(1)} %get-tuple-element.29), kind=kCustom, calls=%fused_computation.18 | custom fusion | bytes 8389120 | tf_op jit(solution)/shard_map/gather | solution.py:13
  24.1 3.1 %gather_fusion.4 = bf16[128,128,128]{2,1,0:T(8,128)(2,1)} fusion(bf16[16,128,128]{2,1,0:T(8,128)(2,1)S(1)} %bitcast.23, s32[1024]{0:T(1024)S(1)} %get-tuple-element.36), kind=kCustom, calls=%fused_computation.4 | custom fusion | bytes 8389120 | tf_op jit(solution)/shard_map/gather | solution.py:13
  27.2 3.1 %gather_fusion.8 = bf16[128,128,128]{2,1,0:T(8,128)(2,1)} fusion(bf16[16,128,128]{2,1,0:T(8,128)(2,1)S(1)} %bitcast.25, s32[1024]{0:T(1024)S(1)} %get-tuple-element.34), kind=kCustom, calls=%fused_computation.8 | custom fusion | bytes 8389120 | tf_op jit(solution)/shard_map/gather | solution.py:13
  30.3 3.1 %gather_fusion.12 = bf16[128,128,128]{2,1,0:T(8,128)(2,1)} fusion(bf16[16,128,128]{2,1,0:T(8,128)(2,1)S(1)} %bitcast.27, s32[1024]{0:T(1024)S(1)} %get-tuple-element.32), kind=kCustom, calls=%fused_computation.12 | custom fusion | bytes 8389120 | tf_op jit(solution)/shard_map/gather | solution.py:13
  33.4 3.0 %gather_fusion.16 = bf16[128,128,128]{2,1,0:T(8,128)(2,1)} fusion(bf16[16,128,128]{2,1,0:T(8,128)(2,1)S(1)} %bitcast.29, s32[1024]{0:T(1024)S(1)} %get-tuple-element.30), kind=kCustom, calls=%fused_computation.16 | custom fusion | bytes 8389120 | tf_op jit(solution)/shard_map/gather | solution.py:13
  36.5 0.4 fusion.14
  36.9 88.8 %all-gather.3.cloned.1.call-done = bf16[1,1,256,128,128]{4,3,1,0,2:T(8,128)(2,1)} async-done(((bf16[1,1,16,128,128]{4,3,1,0,2:T(8,128)(2,1)}), bf16[1,1,256,128,128]{4,3,1,0,2:T(8,128)(2,1)}) %all-gather.3.cloned.1.call-update) | async-done | bytes 8388624 | tf_op jit(solution)/shard_map/all_gather | solution.py:28
  125.7 6.4 %gather_fusion.5 = bf16[128,128,128]{2,1,0:T(8,128)(2,1)} fusion(bf16[256,128,128]{2,1,0:T(8,128)(2,1)} %bitcast.31, s32[1024]{0:T(1024)S(1)} %get-tuple-element.27), kind=kCustom, calls=%fused_computation.5 | custom fusion | bytes 8389120 | tf_op jit(solution)/shard_map/gather | solution.py:12
  132.1 6.4 %gather_fusion.9 = bf16[128,128,128]{2,1,0:T(8,128)(2,1)} fusion(bf16[256,128,128]{2,1,0:T(8,128)(2,1)} %bitcast.32, s32[1024]{0:T(1024)S(1)} %get-tuple-element.25), kind=kCustom, calls=%fused_computation.9 | custom fusion | bytes 8389120 | tf_op jit(solution)/shard_map/gather | solution.py:12
  138.6 6.4 %gather_fusion.13 = bf16[128,128,128]{2,1,0:T(8,128)(2,1)} fusion(bf16[256,128,128]{2,1,0:T(8,128)(2,1)} %bitcast.33, s32[1024]{0:T(1024)S(1)} %get-tuple-element.23), kind=kCustom, calls=%fused_computation.13 | custom fusion | bytes 8389120 | tf_op jit(solution)/shard_map/gather | solution.py:12
  145.0 6.4 %gather_fusion.17 = bf16[128,128,128]{2,1,0:T(8,128)(2,1)} fusion(bf16[256,128,128]{2,1,0:T(8,128)(2,1)} %bitcast.34, s32[1024]{0:T(1024)S(1)} %get-tuple-element.21), kind=kCustom, calls=%fused_computation.17 | custom fusion | bytes 8389120 | tf_op jit(solution)/shard_map/gather | solution.py:12
  151.3 6.4 %gather_fusion.2 = bf16[128,128,128]{2,1,0:T(8,128)(2,1)} fusion(bf16[256,128,128]{2,1,0:T(8,128)(2,1)} %bitcast.35, s32[1024]{0:T(1024)S(1)} %get-tuple-element.28), kind=kCustom, calls=%fused_computation.2 | custom fusion | bytes 8389120 | tf_op jit(solution)/shard_map/gather | solution.py:12
  157.8 6.4 %gather_fusion.7 = bf16[128,128,128]{2,1,0:T(8,128)(2,1)} fusion(bf16[256,128,128]{2,1,0:T(8,128)(2,1)} %bitcast.36, s32[1024]{0:T(1024)S(1)} %get-tuple-element.26), kind=kCustom, calls=%fused_computation.7 | custom fusion | bytes 8389120 | tf_op jit(solution)/shard_map/gather | solution.py:12
  164.2 6.4 %gather_fusion.11 = bf16[128,128,128]{2,1,0:T(8,128)(2,1)} fusion(bf16[256,128,128]{2,1,0:T(8,128)(2,1)} %bitcast.37, s32[1024]{0:T(1024)S(1)} %get-tuple-element.24), kind=kCustom, calls=%fused_computation.11 | custom fusion | bytes 8389120 | tf_op jit(solution)/shard_map/gather | solution.py:12
  170.6 6.4 %gather_fusion.15 = bf16[128,128,128]{2,1,0:T(8,128)(2,1)} fusion(bf16[256,128,128]{2,1,0:T(8,128)(2,1)} %bitcast.38, s32[1024]{0:T(1024)S(1)} %get-tuple-element.22), kind=kCustom, calls=%fused_computation.15 | custom fusion | bytes 8389120 | tf_op jit(solution)/shard_map/gather | solution.py:12
  177.0 0.0 copy-start.3
  177.0 0.0 copy-start.11
  177.0 8.1 %fusion.17 = f32[128,128,128]{2,1,0:T(8,128)} fusion(bf16[128,128,128]{2,1,0:T(8,128)(2,1)} %gather_fusion.5, bf16[128,128,128]{2,1,0:T(8,128)(2,1)} %gather_fusion.6), kind=kOutput, calls=%fused_computation.71 | convolution fusion | flops 536870912 | bytes 16777216 | tf_op jit(solution)/shard_map/pij,pjk->pik/dot_general | solution.py:10
  185.0 0.0 copy-done.3
  185.0 0.0 copy-done.11
  185.0 0.0 copy-start.4
  185.0 0.0 copy-start.10
  185.1 5.4 %fusion.19 = f32[128,128,128]{2,1,0:T(8,128)} fusion(bf16[128,128,128]{2,1,0:T(8,128)(2,1)S(1)} %copy-done.11, bf16[128,128,128]{2,1,0:T(8,128)(2,1)S(1)} %copy-done.3), kind=kOutput, calls=%fused_computation.73 | convolution fusion | flops 536870912 | bytes 16777216 | tf_op jit(solution)/shard_map/pij,pjk->pik/dot_general | solution.py:10
  190.5 0.0 copy-done.4
  190.5 0.4 copy-done.10
  190.9 0.0 copy-start.6
  190.9 0.0 copy-start.12
  190.9 5.5 %fusion.21 = f32[128,128,128]{2,1,0:T(8,128)} fusion(bf16[128,128,128]{2,1,0:T(8,128)(2,1)S(1)} %copy-done.10, bf16[128,128,128]{2,1,0:T(8,128)(2,1)S(1)} %copy-done.4), kind=kOutput, calls=%fused_computation.75 | convolution fusion | flops 536870912 | bytes 16777216 | tf_op jit(solution)/shard_map/pij,pjk->pik/dot_general | solution.py:10
  196.4 0.0 copy-done.6
  196.4 0.9 copy-done.12
  197.4 0.0 copy-start.7
  197.4 0.0 copy-start.13
  197.4 5.5 %fusion.16 = f32[128,128,128]{2,1,0:T(8,128)} fusion(bf16[128,128,128]{2,1,0:T(8,128)(2,1)S(1)} %copy-done.12, bf16[128,128,128]{2,1,0:T(8,128)(2,1)S(1)} %copy-done.6), kind=kOutput, calls=%fused_computation.70 | convolution fusion | flops 536870912 | bytes 16777216 | tf_op jit(solution)/shard_map/pij,pjk->pik/dot_general | solution.py:10
  202.8 0.0 copy-done.7
  202.8 0.9 copy-done.13
  203.8 0.0 copy-start.8
  203.8 0.0 copy-start.14
  203.8 5.5 %fusion.18 = f32[128,128,128]{2,1,0:T(8,128)} fusion(bf16[128,128,128]{2,1,0:T(8,128)(2,1)S(1)} %copy-done.13, bf16[128,128,128]{2,1,0:T(8,128)(2,1)S(1)} %copy-done.7), kind=kOutput, calls=%fused_computation.72 | convolution fusion | flops 536870912 | bytes 16777216 | tf_op jit(solution)/shard_map/pij,pjk->pik/dot_general | solution.py:10
  209.3 0.0 copy-done.8
  209.3 0.9 copy-done.14
  210.2 5.5 %fusion.22 = f32[128,128,128]{2,1,0:T(8,128)} fusion(bf16[128,128,128]{2,1,0:T(8,128)(2,1)S(1)} %copy-done.14, bf16[128,128,128]{2,1,0:T(8,128)(2,1)S(1)} %copy-done.8), kind=kOutput, calls=%fused_computation.76 | convolution fusion | flops 536870912 | bytes 16777216 | tf_op jit(solution)/shard_map/pij,pjk->pik/dot_general | solution.py:10
  215.7 0.0 copy-done.5
  215.7 0.9 copy-done.9
  216.6 4.5 %fusion.20 = f32[128,128,128]{2,1,0:T(8,128)} fusion(bf16[128,128,128]{2,1,0:T(8,128)(2,1)S(1)} %copy-done.9, bf16[128,128,128]{2,1,0:T(8,128)(2,1)S(1)} %copy-done.5), kind=kOutput, calls=%fused_computation.74 | convolution fusion | flops 536870912 | bytes 16777216 | tf_op jit(solution)/shard_map/pij,pjk->pik/dot_general | solution.py:10
  221.1 0.0 copy-done.2
  221.1 22.7 %add_convert_fusion = bf16[128,128,128]{2,1,0:T(8,128)(2,1)} fusion(f32[128,128,128]{2,1,0:T(8,128)} %fusion.22, f32[128,128,128]{2,1,0:T(8,128)} %fusion.21, f32[128,128,128]{2,1,0:T(8,128)} %fusion.20, f32[128,128,128]{2,1,0:T(8,128)} %fusion.19, f32[128,128,128]{2,1,0:T(8,128)} %fusion.18, f32[128,128,128]{2,1,0:T(8,128)} %fusion.16, ...), kind=kOutput, calls=%fused_computation.19 | convolution fusion | flops 553648128 | bytes 71303168 | tf_op jit(solution)/shard_map/pij,pjk->pik/dot_general | solution.py:10
  243.8 0.0 reduce-scatter.2.cloned.1.call-update
  243.8 10.4 %reduce-scatter.2.cloned.1.call-done = bf16[64,128,128]{2,1,0:T(8,128)(2,1)} async-done(((bf16[128,128,128]{2,1,0:T(8,128)(2,1)}), bf16[64,128,128]{2,1,0:T(8,128)(2,1)}) %reduce-scatter.2.cloned.1.call-update) | async-done | bytes 2097168 | tf_op jit(solution)/shard_map/reduce_scatter | solution.py:36
  254.2 0.0 copy-done.1
  (15 shorter events, 0.1 us)
Async XLA Ops:
  6.5 5.5 %copy-start = (bf16[1,1,16,128,128]{4,3,2,1,0:T(8,128)(2,1)S(1)}, bf16[1,1,16,128,128]{4,3,2,1,0:T(8,128)(2,1)}, u32[]{:S(2)}) copy-start(bf16[1,1,16,128,128]{4,3,2,1,0:T(8,128)(2,1)} %param.6) | copy-start | bytes 1572868
  6.5 119.2 %all-gather.3.cloned.1.call-start = ((), (), s32[]{:S(2)}) async-start(), calls=%async_computation.2 | async-start | bytes 8912896 | tf_op jit(solution)/shard_map/all_gather | solution.py:28
  7.3 246.9 %reduce-scatter.2.cloned.1.call-start = ((), (), s32[]{:S(2)}) async-start(), calls=%async_computation.1 | async-start | bytes 6291456 | tf_op jit(solution)/shard_map/reduce_scatter | solution.py:36
  177.0 8.1 %copy-start.3 = (bf16[128,128,128]{2,1,0:T(8,128)(2,1)S(1)}, bf16[128,128,128]{2,1,0:T(8,128)(2,1)}, u32[]{:S(2)}) copy-start(bf16[128,128,128]{2,1,0:T(8,128)(2,1)} %gather_fusion.10) | copy-start | bytes 12582916
  177.0 8.1 %copy-start.11 = (bf16[128,128,128]{2,1,0:T(8,128)(2,1)S(1)}, bf16[128,128,128]{2,1,0:T(8,128)(2,1)}, u32[]{:S(2)}) copy-start(bf16[128,128,128]{2,1,0:T(8,128)(2,1)} %gather_fusion.9) | copy-start | bytes 12582916
  185.0 5.4 %copy-start.4 = (bf16[128,128,128]{2,1,0:T(8,128)(2,1)S(1)}, bf16[128,128,128]{2,1,0:T(8,128)(2,1)}, u32[]{:S(2)}) copy-start(bf16[128,128,128]{2,1,0:T(8,128)(2,1)} %gather_fusion.14) | copy-start | bytes 12582916
  185.0 5.9 %copy-start.10 = (bf16[128,128,128]{2,1,0:T(8,128)(2,1)S(1)}, bf16[128,128,128]{2,1,0:T(8,128)(2,1)}, u32[]{:S(2)}) copy-start(bf16[128,128,128]{2,1,0:T(8,128)(2,1)} %gather_fusion.13) | copy-start | bytes 12582916
  190.9 5.5 %copy-start.6 = (bf16[128,128,128]{2,1,0:T(8,128)(2,1)S(1)}, bf16[128,128,128]{2,1,0:T(8,128)(2,1)}, u32[]{:S(2)}) copy-start(bf16[128,128,128]{2,1,0:T(8,128)(2,1)} %gather_fusion.4) | copy-start | bytes 12582916
  190.9 6.4 %copy-start.12 = (bf16[128,128,128]{2,1,0:T(8,128)(2,1)S(1)}, bf16[128,128,128]{2,1,0:T(8,128)(2,1)}, u32[]{:S(2)}) copy-start(bf16[128,128,128]{2,1,0:T(8,128)(2,1)} %gather_fusion.2) | copy-start | bytes 12582916
  197.4 5.5 %copy-start.7 = (bf16[128,128,128]{2,1,0:T(8,128)(2,1)S(1)}, bf16[128,128,128]{2,1,0:T(8,128)(2,1)}, u32[]{:S(2)}) copy-start(bf16[128,128,128]{2,1,0:T(8,128)(2,1)} %gather_fusion.8) | copy-start | bytes 12582916
  197.4 6.4 %copy-start.13 = (bf16[128,128,128]{2,1,0:T(8,128)(2,1)S(1)}, bf16[128,128,128]{2,1,0:T(8,128)(2,1)}, u32[]{:S(2)}) copy-start(bf16[128,128,128]{2,1,0:T(8,128)(2,1)} %gather_fusion.7) | copy-start | bytes 12582916
  203.8 5.5 %copy-start.8 = (bf16[128,128,128]{2,1,0:T(8,128)(2,1)S(1)}, bf16[128,128,128]{2,1,0:T(8,128)(2,1)}, u32[]{:S(2)}) copy-start(bf16[128,128,128]{2,1,0:T(8,128)(2,1)} %gather_fusion.16) | copy-start | bytes 12582916
  203.8 6.4 %copy-start.14 = (bf16[128,128,128]{2,1,0:T(8,128)(2,1)S(1)}, bf16[128,128,128]{2,1,0:T(8,128)(2,1)}, u32[]{:S(2)}) copy-start(bf16[128,128,128]{2,1,0:T(8,128)(2,1)} %gather_fusion.15) | copy-start | bytes 12582916
  210.2 5.5 %copy-start.5 = (bf16[128,128,128]{2,1,0:T(8,128)(2,1)S(1)}, bf16[128,128,128]{2,1,0:T(8,128)(2,1)}, u32[]{:S(2)}) copy-start(bf16[128,128,128]{2,1,0:T(8,128)(2,1)} %gather_fusion.12) | copy-start | bytes 12582916
  210.2 6.4 %copy-start.9 = (bf16[128,128,128]{2,1,0:T(8,128)(2,1)S(1)}, bf16[128,128,128]{2,1,0:T(8,128)(2,1)}, u32[]{:S(2)}) copy-start(bf16[128,128,128]{2,1,0:T(8,128)(2,1)} %gather_fusion.11) | copy-start | bytes 12582916
  216.6 4.5 %copy-start.2 = (bf16[128,128,128]{2,1,0:T(8,128)(2,1)S(1)}, bf16[128,128,128]{2,1,0:T(8,128)(2,1)}, u32[]{:S(2)}) copy-start(bf16[128,128,128]{2,1,0:T(8,128)(2,1)} %gather_fusion.18) | copy-start | bytes 12582916
  221.1 33.1 %copy-start.1 = (bf16[1,1,16,128,128]{4,3,2,1,0:T(8,128)(2,1)S(1)}, bf16[1,1,16,128,128]{4,3,2,1,0:T(8,128)(2,1)}, u32[]{:S(2)}) copy-start(bf16[1,1,16,128,128]{4,3,2,1,0:T(8,128)(2,1)} %param.6) | copy-start | bytes 1572868
Sparse Core Ops, SparseCore 0:
  10.1 115.5 all-gather.2
  243.9 10.2 reduce-scatter.1
where the time goes:
time: 261 us
  waiting for transfers between devices  99.9 us (38%)
  local copies, waits for them, and re-layouts  84.2 us (32%)
  matrix products  62.5 us (24%)
  between operations  13.5 us (5%)
    all_gather x1, waiting for transfers between devices, on_device(): row_panel = lax.all_gather(x_local, 'col', axis=0, tiled=True)  88.8 us
    dot_general x8, matrix products, block_terms(): jnp.einsum('pij,pjk->pik', row_panel[left_list[:, term]], col_panel[b_lis...  62.5 us
    gather x8, local copies, waits for them, and re-layouts, block_terms(): row_panel[left_list[:, term]]  51.3 us
    gather x8, local copies, waits for them, and re-layouts, block_terms(): col_panel[b_list[:, term]]  24.4 us
    reduce_scatter x1, waiting for transfers between devices, on_device(): lax.psum_scatter(partial_value.astype(jnp.bfloat16), 'layer', scatter_dim...  10.4 us
    unnamed x33, local copies, waits for them, and re-layouts  6.63 us
  transfers between devices with their start and end apart: 2, of which 2 were waited for; matrix products, arithmetic and copies ran while one was open for 11% of the time, Pallas kernels for 0%

commit v1 on v0

v1 whole, which is shorter than its diff:
```python
import functools

import jax
import jax.numpy as jnp
from jax import lax
from jax.experimental import pallas as pl
from jax.experimental.pallas import tpu as pltpu
from jax.sharding import PartitionSpec as P


def product_kernel(rows, keep, src_ref, off_ref, slot_ref, panel_ref, h_ref, out_ref):
    per_src = panel_ref.shape[1]
    terms = src_ref.shape[1]
    layer = lax.axis_index("layer")
    start = (layer if keep else 1 - layer) * rows

    @pl.loop(0, rows, unroll=4)
    def _(p):
        row = start + p
        left = [panel_ref[src_ref[row, k], off_ref[row, k]] for k in range(terms)]
        right = [h_ref[slot_ref[row, k]] for k in range(terms)]
        out_ref[p] = jnp.dot(
            jnp.concatenate(left, axis=1),
            jnp.concatenate(right, axis=0),
            preferred_element_type=jnp.float32,
        ).astype(out_ref.dtype)


def products(keep, src, off, slot, panel, h):
    rows = src.shape[0] // 2
    bs = h.shape[-1]
    smem = pl.BlockSpec(memory_space=pltpu.SMEM)
    vmem = pl.BlockSpec(memory_space=pltpu.VMEM)
    return pl.pallas_call(
        functools.partial(product_kernel, rows, keep),
        out_shape=jax.ShapeDtypeStruct((rows, bs, bs), jnp.bfloat16),
        in_specs=[smem, smem, smem, vmem, vmem],
        out_specs=vmem,
        compiler_params=pltpu.CompilerParams(vmem_limit_bytes=40 << 20),
        cost_estimate=pl.CostEstimate(
            flops=2 * rows * src.shape[1] * bs**3,
            bytes_accessed=panel.size * 2 + h.size * 2 + rows * bs * bs * 2,
            transcendentals=0,
        ),
    )(src, off, slot, panel, h)


def on_device(x_blocks, h_blocks, a_src, a_off, b_slot):
    x_local = x_blocks[0, 0]
    h = lax.all_gather(h_blocks[0, 0], "row", axis=0, tiled=True)
    panel = lax.all_gather(x_local, "col", axis=0, tiled=False)
    lists = (a_src[0, 0, 0], a_off[0, 0, 0], b_slot[0, 0, 0])
    theirs = products(False, *lists, panel, h)
    arrived = lax.ppermute(theirs, "layer", [(0, 1), (1, 0)])
    mine = products(True, *lists, panel, h)
    total = mine.astype(jnp.float32) + arrived.astype(jnp.float32)
    return total.astype(jnp.bfloat16)[None, None]


def solution(mesh):
    placed = P("row", "col", "layer", None, None)
    return jax.shard_map(
        on_device,
        mesh=mesh,
        in_specs=(placed,) * 5,
        out_specs=placed,
        check_vma=False,
    )
```

time: 261 us -> 161 us (0.62)
  local copies, waits for them, and re-layouts: 84.2 us -> 6.78 us
  matrix products: 62.5 us -> 0 us
  Pallas kernels: 0 us -> 21.3 us
  waiting for transfers between devices: 99.9 us -> 117 us
    gather x19 -> x0, local copies, waits for them, and re-layouts: 77.6 us -> none  [the longest x8 51.3 us: block_terms(): row_panel[left_list[:, term]]]
    dot_general x8 -> x0, matrix products: 62.5 us -> none  [block_terms(): jnp.einsum('pij,pjk->pik', row_panel[left_list[:, term]], col_panel[b_lis...]
    all_gather x1, waiting for transfers between devices: 88.8 us -> 116 us  [on_device(): panel = lax.all_gather(x_local, 'col', axis=0, tiled=False)]
    pallas_call x0 -> x2, Pallas kernels: none -> 21.3 us  [products(): pl.pallas_call(functools.partial(product_kernel, rows, keep), out_shape=j...]
    reduce_scatter x1 -> x0, waiting for transfers between devices: 10.4 us -> none  [on_device(): lax.psum_scatter(partial_value.astype(jnp.bfloat16), 'layer', scatter_dim...]
    unnamed x33 -> x7, local copies, waits for them, and re-layouts: 6.63 us -> 6.78 us
  transfers between devices with their start and end apart: 2 -> 2, of which waited for: 2 -> 1; matrix products, arithmetic and copies ran while one was open for 11% -> 1% of each run, Pallas kernels for 0% -> 7%
where the time goes in v1:
time: 161 us
  waiting for transfers between devices  117 us (73%)
  Pallas kernels  21.3 us (13%)
  between operations  13.4 us (8%)
  local copies, waits for them, and re-layouts  6.78 us (4%)
  other arithmetic  2.42 us (2%)
    all_gather x1, waiting for transfers between devices, on_device(): panel = lax.all_gather(x_local, 'col', axis=0, tiled=False)  116 us
    pallas_call x2, Pallas kernels, products(): pl.pallas_call(functools.partial(product_kernel, rows, keep), out_shape=j...  21.3 us
    unnamed x7, local copies, waits for them, and re-layouts  6.78 us
  transfers between devices with their start and end apart: 2, of which 1 were waited for; matrix products, arithmetic and copies ran while one was open for 1% of the time, Pallas kernels for 7%

profile of v1, /device:TPU:0, one launch (start us, length us, event | category | flops | bytes accessed | tf_op | source)
XLA Modules:
  0.0 160.8 jit_solution(10908227848148635797)
XLA Ops:
  6.5 0.0 all-gather.3.cloned.1.call-start
  6.5 0.7 all-gather.3.cloned.1.call-update
  7.3 0.8 copy.10
  8.0 0.8 copy.11
  8.8 0.8 copy.12
  9.6 116.1 %all-gather.3.cloned.1.call-done = bf16[16,1,16,128,128]{4,3,2,1,0:T(8,128)(2,1)} async-done(((bf16[1,1,16,128,128]{4,3,2,1,0:T(8,128)(2,1)}), bf16[16,1,16,128,128]{4,3,2,1,0:T(8,128)(2,1)}) %all-gather.3.cloned.1.call-update) | async-done | bytes 8388624 | tf_op jit(solution)/shard_map/all_gather | solution.py:51
  125.7 0.0 copy-start
  125.7 3.4 %copy-done = bf16[16,1,16,128,128]{4,3,2,1,0:T(8,128)(2,1)S(1)} copy-done((bf16[16,1,16,128,128]{4,3,2,1,0:T(8,128)(2,1)S(1)}, bf16[16,1,16,128,128]{4,3,2,1,0:T(8,128)(2,1)}, u32[]{:S(2)}) %copy-start) | copy-done | bytes 8388632
  129.1 0.0 copy-start.1
  129.1 1.0 copy-done.1
  130.1 10.6 %shard_map.56 = bf16[64,128,128]{2,1,0:T(8,128)(2,1)S(1)} custom-call(s32[128,8]{1,0:T(8,128)S(1)} %bitcast.11, s32[128,8]{1,0:T(8,128)S(1)} %bitcast.13, s32[128,8]{1,0:T(8,128)S(1)} %bitcast.15, bf16[16,16,128,128]{3,2,1,0:T(8,128)(2,1)S(1)} %bitcast.7, bf16[16,128,128]{2,1,0:T(8,128)(2,1)S(1)} %bitcast.9), custom_call_target="tpu_custom_call" | custom-call | flops 2147483648 | bytes 11010048 | tf_op jit(solution)/shard_map/pallas_call | solution.py:34
  140.8 0.1 collective-permute-start
  140.8 10.6 %shard_map.55 = bf16[64,128,128]{2,1,0:T(8,128)(2,1)S(1)} custom-call(s32[128,8]{1,0:T(8,128)S(1)} %bitcast.12, s32[128,8]{1,0:T(8,128)S(1)} %bitcast.14, s32[128,8]{1,0:T(8,128)S(1)} %bitcast.16, bf16[16,16,128,128]{3,2,1,0:T(8,128)(2,1)S(1)} %bitcast.8, bf16[16,128,128]{2,1,0:T(8,128)(2,1)S(1)} %bitcast.10), custom_call_target="tpu_custom_call" | custom-call | flops 2147483648 | bytes 11010048 | tf_op jit(solution)/shard_map/pallas_call | solution.py:34
  151.5 0.0 collective-permute-done
  151.5 2.4 %fusion = bf16[1,1,64,128,128]{4,3,2,1,0:T(8,128)(2,1)} fusion(bf16[64,128,128]{2,1,0:T(8,128)(2,1)S(1)} %collective-permute-done, bf16[64,128,128]{2,1,0:T(8,128)(2,1)S(1)} %shard_map.55), kind=kLoop, calls=%fused_computation.1 | loop fusion | flops 4194304 | bytes 6291456 | tf_op jit(solution)/shard_map/broadcast_in_dim | solution.py:57
Async XLA Ops:
  6.5 119.2 %all-gather.3.cloned.1.call-start = ((), (), s32[]{:S(2)}) async-start(), calls=%async_computation | async-start | bytes 8912896 | tf_op jit(solution)/shard_map/all_gather | solution.py:51
  125.7 3.4 %copy-start = (bf16[16,1,16,128,128]{4,3,2,1,0:T(8,128)(2,1)S(1)}, bf16[16,1,16,128,128]{4,3,2,1,0:T(8,128)(2,1)}, u32[]{:S(2)}) copy-start(bf16[16,1,16,128,128]{4,3,2,1,0:T(8,128)(2,1)} %all-gather.3.cloned.1.call-done) | copy-start | bytes 25165828
  129.1 1.0 copy-start.1
  140.8 10.7 %collective-permute-start = (bf16[64,128,128]{2,1,0:T(8,128)(2,1)S(1)}, bf16[64,128,128]{2,1,0:T(8,128)(2,1)S(1)}, u32[]{:S(2)}, u32[]{:S(2)}) collective-permute-start(bf16[64,128,128]{2,1,0:T(8,128)(2,1)S(1)} %shard_map.56), channel_id=1, source_target_pairs={{0,16},{16,0},{1,17},{17,1},{2,18},{18,2},{3,19},{19,3},{4,20},{20... | collective-permute-start | bytes 6291464 | tf_op jit(solution)/shard_map/ppermute | solution.py:54
Sparse Core Ops, SparseCore 0:
  10.1 115.5 all-gather.2

commit v2 on v1

v2 whole, which is shorter than its diff:
```python
import functools
import itertools

import jax
import jax.numpy as jnp
from jax import lax
from jax.experimental import pallas as pl
from jax.experimental.pallas import tpu as pltpu
from jax.sharding import PartitionSpec as P

CHUNKS = 8
ORDERS = (((0, 2, 1), 4), ((1, 2, 0), 4), ((2, 0, 1), 4), ((2, 1, 0), 4))


def line_sizes(cols):
    x = 2
    z = 4 if cols % 8 == 0 else 1
    return (x, cols // (x * z), z)


def shares(blocks):
    found, low = [], 0
    for order, part in ORDERS:
        high = low + max(1, blocks * part // 16)
        found.append((order, low, high))
        low = high
    return tuple(found)


def steps_of(size):
    found = [0]
    for far in range(1, size):
        found += [far] if size == 2 else [far, -far]
    return found


class Spread:
    def __init__(self, x_ref, panel, send_sem, recv_sem):
        self.x_ref, self.panel, self.send_sem, self.recv_sem = x_ref, panel, send_sem, recv_sem
        self.sizes = line_sizes(panel.shape[0])
        self.parts = shares(panel.shape[1])
        self.me = lax.axis_index("col")
        rest, self.at = self.me, []
        for size in self.sizes:
            self.at.append(lax.rem(rest, size))
            rest = lax.div(rest, size)

    def index(self, at):
        return (at[2] * self.sizes[1] + at[1]) * self.sizes[0] + at[0]

    def source(self, rel):
        at, ok = [], None
        for here, step, size in zip(self.at, rel, self.sizes):
            if size == 2:
                at.append(lax.rem(here + step, 2))
            else:
                at.append(here + step)
                if step:
                    inside = here + step < size if step > 0 else here + step >= 0
                    ok = inside if ok is None else jnp.logical_and(ok, inside)
        return at, ok

    def ways(self, dim):
        size = self.sizes[dim]
        if size == 1:
            return []
        stride = 1
        for other in self.sizes[:dim]:
            stride *= other
        here = self.at[dim]
        if size == 2:
            return [(2 * dim, self.me + (1 - 2 * here) * stride, None, 0)]
        return [
            (2 * dim, self.me + stride, here + 1 < size, 1),
            (2 * dim + 1, self.me - stride, here >= 1, -1),
        ]

    def greet(self):
        barrier = pltpu.get_barrier_semaphore()
        count = 0
        for dim in range(3):
            for _, other, ok, _ in self.ways(dim):
                def hail(other=other):
                    pl.semaphore_signal(
                        barrier, inc=1, device_id={"col": other}, device_id_type=pl.DeviceIdType.MESH
                    )
                if ok is None:
                    hail()
                    count = count + 1
                else:
                    pl.when(ok)(hail)
                    count = count + ok.astype(jnp.int32)
        return barrier, count

    def copy(self, part, own, src, slot, other):
        _, low, high = self.parts[part]
        blocks = pl.ds(low, high - low)
        return pltpu.make_async_remote_copy(
            src_ref=self.x_ref.at[blocks] if own else self.panel.at[src, blocks],
            dst_ref=self.panel.at[src, blocks],
            send_sem=self.send_sem.at[part, src, slot],
            recv_sem=self.recv_sem.at[part, src],
            device_id={"col": other},
            device_id_type=pl.DeviceIdType.MESH,
        )

    def onward(self, part, rel):
        order = self.parts[part][0]
        moved = [place for place in range(3) if rel[order[place]]]
        last = moved[-1] if moved else -1
        found = []
        if moved:
            dim = order[last]
            if self.sizes[dim] > 2:
                found += [way for way in self.ways(dim) if way[3] * rel[dim] < 0]
        for place in range(last + 1, 3):
            found += self.ways(order[place])
        return found

    def events(self):
        rels = itertools.product(*(steps_of(size) for size in self.sizes))
        found = [
            (part, rel)
            for rel in rels
            for part in range(len(self.parts))
        ]
        def when(event):
            part, rel = event
            order = self.parts[part][0]
            hops = sum(abs(step) for step in rel)
            final = rel[order[2]] != 0 and self.sizes[order[2]] == 2
            return (final, hops, abs(rel[2]), part)
        return sorted(found, key=when)

    def visit(self, part, rel, act):
        at, ok = self.source(rel)
        src = self.index(at)
        def body():
            act(src)
        if ok is None:
            body()
        else:
            pl.when(ok)(body)

    def start_onward(self, part, rel, src):
        own = not any(rel)
        for slot, other, ok, _ in self.onward(part, rel):
            send = self.copy(part, own, src, slot, other).start
            if ok is None:
                send()
            else:
                pl.when(ok)(send)

    def wait_sent(self, part, rel, src):
        own = not any(rel)
        for slot, other, ok, _ in self.onward(part, rel):
            wait = self.copy(part, own, src, slot, other).wait_send
            if ok is None:
                wait()
            else:
                pl.when(ok)(wait)

    def run(self):
        for part, rel in self.events():
            def act(src, part=part, rel=rel):
                if any(rel):
                    self.copy(part, False, src, 0, self.ways(0)[0][1]).wait_recv()
                self.start_onward(part, rel, src)
            self.visit(part, rel, act)

    def finish(self):
        for part, rel in self.events():
            self.visit(part, rel, lambda src, part=part, rel=rel: self.wait_sent(part, rel, src))


def kernel(
    code_ref, x_ref, h_ref, out_ref,
    panel, theirs, arrived, own_sem, send_sem, recv_sem, swap_send, swap_recv,
):
    layer = lax.axis_index("layer")
    rows, terms = code_ref.shape
    keep = rows // 2
    slots = h_ref.shape[0]
    per_src = x_ref.shape[0]
    spread = Spread(x_ref, panel, send_sem, recv_sem)
    barrier, count = spread.greet()
    pl.semaphore_signal(
        barrier, inc=1, device_id={"layer": 1 - layer}, device_id_type=pl.DeviceIdType.MESH
    )
    local = pltpu.make_async_copy(x_ref, panel.at[spread.me], own_sem)
    local.start()
    pl.semaphore_wait(barrier, count + 1)
    spread.run()
    local.wait()

    def product(row):
        left, right = [], []
        for k in range(terms):
            code = code_ref[row, k]
            block = lax.div(code, slots)
            left.append(panel[lax.div(block, per_src), lax.rem(block, per_src)])
            right.append(h_ref[lax.rem(code, slots)])
        return jnp.dot(
            jnp.concatenate(left, axis=1),
            jnp.concatenate(right, axis=0),
            preferred_element_type=jnp.float32,
        ).astype(jnp.bfloat16)

    size = keep // CHUNKS

    def swap(chunk):
        part = pl.ds(chunk * size, size)
        return pltpu.make_async_remote_copy(
            src_ref=theirs.at[part],
            dst_ref=arrived.at[part],
            send_sem=swap_send.at[chunk],
            recv_sem=swap_recv.at[chunk],
            device_id={"layer": 1 - layer},
            device_id_type=pl.DeviceIdType.MESH,
        )

    @pl.loop(0, CHUNKS)
    def _(chunk):
        @pl.loop(0, size, unroll=4)
        def _(i):
            p = chunk * size + i
            theirs[p] = product((1 - layer) * keep + p)
        swap(chunk).start()

    @pl.loop(0, CHUNKS)
    def _(chunk):
        swap(chunk).wait_recv()

        @pl.loop(0, size, unroll=4)
        def _(i):
            p = chunk * size + i
            total = product(layer * keep + p).astype(jnp.float32) + arrived[p].astype(jnp.float32)
            out_ref[p] = total.astype(out_ref.dtype)

    spread.finish()

    @pl.loop(0, CHUNKS)
    def _(chunk):
        swap(chunk).wait_send()


def on_device(cols, x_blocks, h_blocks, a_src, a_off, b_slot):
    x_local = x_blocks[0, 0]
    h = lax.all_gather(h_blocks[0, 0], "row", axis=0, tiled=True)
    per_src, bs = x_local.shape[0], x_local.shape[1]
    rows = a_src.shape[3]
    slots = h.shape[0]
    code = ((a_src * per_src + a_off) * slots + b_slot)[0, 0, 0]
    parts = len(shares(per_src))
    vmem = pl.BlockSpec(memory_space=pltpu.VMEM)
    out = pl.pallas_call(
        kernel,
        out_shape=jax.ShapeDtypeStruct((rows // 2, bs, bs), jnp.bfloat16),
        in_specs=[pl.BlockSpec(memory_space=pltpu.SMEM), vmem, vmem],
        out_specs=vmem,
        scratch_shapes=[
            pltpu.VMEM((cols, per_src, bs, bs), jnp.bfloat16),
            pltpu.VMEM((rows // 2, bs, bs), jnp.bfloat16),
            pltpu.VMEM((rows // 2, bs, bs), jnp.bfloat16),
            pltpu.SemaphoreType.DMA,
            pltpu.SemaphoreType.DMA((parts, cols, 6)),
            pltpu.SemaphoreType.DMA((parts, cols)),
            pltpu.SemaphoreType.DMA((CHUNKS,)),
            pltpu.SemaphoreType.DMA((CHUNKS,)),
        ],
        compiler_params=pltpu.CompilerParams(
            collective_id=0, has_side_effects=True, vmem_limit_bytes=48 << 20
        ),
    )(code, x_local, h)
    return out[None, None]


def solution(mesh):
    placed = P("row", "col", "layer", None, None)
    return jax.shard_map(
        functools.partial(on_device, mesh.shape["col"]),
        mesh=mesh,
        in_specs=(placed,) * 5,
        out_specs=placed,
        check_vma=False,
    )
```

time: 161 us -> 91.1 us (0.57)
  waiting for transfers between devices: 117 us -> 0 us
  Pallas kernels: 21.3 us -> 85 us
  between operations: 13.4 us -> 0.02 us
  other arithmetic: 2.42 us -> 0.7 us
  local copies, waits for them, and re-layouts: 6.78 us -> 5.08 us
    all_gather x1 -> x0, waiting for transfers between devices: 116 us -> none  [on_device(): panel = lax.all_gather(x_local, 'col', axis=0, tiled=False)]
    pallas_call x2 -> x1, Pallas kernels: 21.3 us -> 85 us  [on_device(): pl.pallas_call(kernel, out_shape=jax.ShapeDtypeStruct((rows // 2, bs, bs)...]
    broadcast_in_dim x1 -> x0, other arithmetic: 2.42 us -> none  [on_device(): return total.astype(jnp.bfloat16)[None, None]]
    unnamed x7, local copies, waits for them, and re-layouts: 6.78 us -> 4.97 us
  transfers between devices with their start and end apart: 2 -> 0, of which waited for: 1 -> 0; matrix products, arithmetic and copies ran while one was open for 1% -> 0% of each run, Pallas kernels for 7% -> 0%
where the time goes in v2:
time: 91.1 us; the launch traced here: 90.8 us
  Pallas kernels  85 us (93%)
  local copies, waits for them, and re-layouts  5.08 us (6%)
    pallas_call x1, Pallas kernels, on_device(): pl.pallas_call(kernel, out_shape=jax.ShapeDtypeStruct((rows // 2, bs, bs)...  85 us
    unnamed x7, local copies, waits for them, and re-layouts  4.97 us

profile of v2, /device:TPU:0, one launch (start us, length us, event | category | flops | bytes accessed | tf_op | source)
XLA Modules:
  0.0 90.8 jit_solution(17091843497643721612)
XLA Ops:
  0.0 0.7 broadcast_multiply_fusion
  0.7 0.1 copy.10
  0.8 0.8 copy.11
  1.6 0.8 copy.13
  2.4 0.0 copy-start
  2.4 1.0 %copy-done = bf16[1,1,16,128,128]{4,3,2,1,0:T(8,128)(2,1)S(1)} copy-done((bf16[1,1,16,128,128]{4,3,2,1,0:T(8,128)(2,1)S(1)}, bf16[1,1,16,128,128]{4,3,2,1,0:T(8,128)(2,1)}, u32[]{:S(2)}) %copy-start) | copy-done | bytes 524312
  3.4 0.0 copy-start.1
  3.4 1.0 %copy-done.1 = bf16[1,1,16,128,128]{4,3,2,1,0:T(8,128)(2,1)S(1)} copy-done((bf16[1,1,16,128,128]{4,3,2,1,0:T(8,128)(2,1)S(1)}, bf16[1,1,16,128,128]{4,3,2,1,0:T(8,128)(2,1)}, u32[]{:S(2)}) %copy-start.1) | copy-done | bytes 524312
  4.5 85.0 %shard_map.55 = bf16[64,128,128]{2,1,0:T(8,128)(2,1)S(1)} custom-call(s32[128,8]{1,0:T(8,128)S(1)} %add_bitcast_fusion.code_ref, bf16[16,128,128]{2,1,0:T(8,128)(2,1)S(1)} %bitcast.6, bf16[16,128,128]{2,1,0:T(8,128)(2,1)S(1)} %bitcast.7), custom_call_target="tpu_custom_call" | custom-call | tf_op jit(solution)/shard_map/pallas_call | solution.py:256
  89.5 1.3 %copy.15 = bf16[1,1,64,128,128]{4,3,2,1,0:T(8,128)(2,1)} copy(bf16[1,1,64,128,128]{4,3,2,1,0:T(8,128)(2,1)S(1)} %bitcast.5) | data formatting | bytes 4194304
  (1 shorter events, 0.0 us)
Async XLA Ops:
  2.4 1.0 %copy-start = (bf16[1,1,16,128,128]{4,3,2,1,0:T(8,128)(2,1)S(1)}, bf16[1,1,16,128,128]{4,3,2,1,0:T(8,128)(2,1)}, u32[]{:S(2)}) copy-start(bf16[1,1,16,128,128]{4,3,2,1,0:T(8,128)(2,1)} %param.5) | copy-start | bytes 1572868
  3.4 1.0 %copy-start.1 = (bf16[1,1,16,128,128]{4,3,2,1,0:T(8,128)(2,1)S(1)}, bf16[1,1,16,128,128]{4,3,2,1,0:T(8,128)(2,1)}, u32[]{:S(2)}) copy-start(bf16[1,1,16,128,128]{4,3,2,1,0:T(8,128)(2,1)} %param.6) | copy-start | bytes 1572868

commit v3 on v2

v3 whole, which is shorter than its diff:
```python
import functools
import itertools

import jax
import jax.numpy as jnp
from jax import lax
from jax.experimental import pallas as pl
from jax.experimental.pallas import tpu as pltpu
from jax.sharding import PartitionSpec as P

CHUNKS = 8
STAGES = (8,)
ORDERS = (((0, 2, 1), 4), ((1, 2, 0), 4), ((2, 0, 1), 4), ((2, 1, 0), 4))


def line_sizes(cols):
    x = 2
    z = 4 if cols % 8 == 0 else 1
    return (x, cols // (x * z), z)


def shares(blocks):
    found, low = [], 0
    for order, part in ORDERS:
        high = low + max(1, blocks * part // 16)
        found.append((order, low, high))
        low = high
    return tuple(found)


def steps_of(size):
    found = [0]
    for far in range(1, size):
        found += [far] if size == 2 else [far, -far]
    return found


def guarded(room, act):
    if room:
        pl.when(functools.reduce(jnp.minimum, room) >= 0)(act)
    else:
        act()


class Spread:
    def __init__(self, x_ref, panel, send_sem, recv_sem):
        self.x_ref, self.panel, self.send_sem, self.recv_sem = x_ref, panel, send_sem, recv_sem
        self.per_src = x_ref.shape[0]
        self.sizes = line_sizes(panel.shape[0] // self.per_src)
        self.parts = shares(self.per_src)
        self.me = lax.axis_index("col")
        rest, self.at = self.me, []
        for size in self.sizes:
            self.at.append(lax.rem(rest, size))
            rest = lax.div(rest, size)

    def index(self, at):
        return (at[2] * self.sizes[1] + at[1]) * self.sizes[0] + at[0]

    def source(self, rel):
        at, room = [], []
        for here, step, size in zip(self.at, rel, self.sizes):
            if size == 2:
                at.append(lax.rem(here + step, 2))
            else:
                at.append(here + step)
                if step:
                    room.append(size - 1 - here - step if step > 0 else here + step)
        return at, room

    def ways(self, dim):
        size = self.sizes[dim]
        if size == 1:
            return []
        stride = 1
        for other in self.sizes[:dim]:
            stride *= other
        here = self.at[dim]
        if size == 2:
            return [(2 * dim, self.me + (1 - 2 * here) * stride, [], 0)]
        return [
            (2 * dim, self.me + stride, [size - 2 - here], 1),
            (2 * dim + 1, self.me - stride, [here - 1], -1),
        ]

    def greet(self):
        barrier = pltpu.get_barrier_semaphore()
        count = 0
        for dim in range(3):
            for _, other, room, _ in self.ways(dim):
                def hail(other=other):
                    pl.semaphore_signal(
                        barrier, inc=1, device_id={"col": other}, device_id_type=pl.DeviceIdType.MESH
                    )
                guarded(room, hail)
                count = count + (jnp.where(room[0] >= 0, 1, 0) if room else 1)
        return barrier, count

    def copy(self, part, own, src, slot, other):
        _, low, high = self.parts[part]
        blocks = pl.ds(low, high - low)
        landing = pl.ds(src * self.per_src + low, high - low)
        return pltpu.make_async_remote_copy(
            src_ref=self.x_ref.at[blocks] if own else self.panel.at[landing],
            dst_ref=self.panel.at[landing],
            send_sem=self.send_sem.at[part, src, slot],
            recv_sem=self.recv_sem.at[part, src],
            device_id={"col": other},
            device_id_type=pl.DeviceIdType.MESH,
        )

    def onward(self, part, rel):
        order = self.parts[part][0]
        moved = [place for place in range(3) if rel[order[place]]]
        last = moved[-1] if moved else -1
        found = []
        if moved:
            dim = order[last]
            if self.sizes[dim] > 2:
                found += [way for way in self.ways(dim) if way[3] * rel[dim] < 0]
        for place in range(last + 1, 3):
            found += self.ways(order[place])
        return found

    def is_final(self, part, far):
        last = self.parts[part][0][2]
        return self.sizes[last] == 2 and far[last] != 0

    def events(self):
        rels = itertools.product(*(steps_of(size) for size in self.sizes))
        found = [(part, rel) for rel in rels for part in range(len(self.parts))]
        return sorted(found, key=lambda e: (sum(map(abs, e[1])), abs(e[1][2]), e[0]))

    def ranked(self):
        nears = itertools.product(*(range(size) for size in self.sizes))
        parts = range(len(self.parts))
        found = []
        for near in sorted(nears, key=lambda n: (sum(self.is_final(q, n) for q in parts), sum(n), n)):
            at = []
            for here, rank, size in zip(self.at, near, self.sizes):
                if size == 2:
                    at.append(lax.rem(here + rank, 2))
                else:
                    place = 0
                    for h in range(size):
                        nearest = sorted(range(size), key=lambda o: (abs(o - h), o))
                        place = place + jnp.where(here == h, nearest[rank], 0)
                    at.append(place)
            found.append((near, self.index(at)))
        return found

    def wait_finals(self, near, src):
        for part in range(len(self.parts)):
            if self.is_final(part, near):
                self.copy(part, False, src, 0, self.ways(0)[0][1]).wait_recv()

    def start_onward(self, part, rel, src):
        own = not any(rel)
        for slot, other, room, _ in self.onward(part, rel):
            guarded(room, self.copy(part, own, src, slot, other).start)

    def run(self):
        for part, rel in self.events():
            if self.is_final(part, rel) or not any(rel):
                continue
            at, room = self.source(rel)
            src = self.index(at)

            def act(src=src, part=part, rel=rel):
                self.copy(part, False, src, 0, self.ways(0)[0][1]).wait_recv()
                self.start_onward(part, rel, src)

            guarded(room, act)

    def finish(self):
        for part, rel in self.events():
            at, room = self.source(rel)
            src = self.index(at)
            for slot, other, more, _ in self.onward(part, rel):
                guarded(room + more, self.copy(part, not any(rel), src, slot, other).wait_send)


def sort_terms(keys, others):
    count = len(keys)
    lists = [list(keys)] + [list(other) for other in others]

    def exchange(i, j):
        swap = lists[0][i] > lists[0][j]
        for each in lists:
            low, high = each[i], each[j]
            each[i], each[j] = jnp.where(swap, high, low), jnp.where(swap, low, high)

    p = 1
    while p < count:
        k = p
        while k >= 1:
            for j in range(k % p, count - k, 2 * k):
                for i in range(min(k, count - j - k)):
                    if (i + j) // (2 * p) == (i + j + k) // (2 * p):
                        exchange(i + j, i + j + k)
            k //= 2
        p *= 2
    return lists[1:]


def kernel(
    src_ref, off_ref, slot_ref, x_ref, h_hbm, out_ref,
    panel, ready, total, h_ref, theirs, arrived, lists, index,
    own_sem, h_sem, index_sem, ready_sem, send_sem, recv_sem, swap_send, swap_recv,
):
    layer = lax.axis_index("layer")
    terms, rows = src_ref.shape
    keep = rows // 2
    per_src = x_ref.shape[0]
    cols = panel.shape[0] // per_src
    spread = Spread(x_ref, panel, send_sem, recv_sem)
    barrier, count = spread.greet()
    pl.semaphore_signal(
        barrier, inc=1, device_id={"layer": 1 - layer}, device_id_type=pl.DeviceIdType.MESH
    )
    local = pltpu.make_async_copy(x_ref, panel.at[pl.ds(spread.me * per_src, per_src)], own_sem)
    local.start()
    load_h = pltpu.make_async_copy(h_hbm, h_ref, h_sem)
    load_h.start()
    ranked = spread.ranked()
    pl.semaphore_wait(barrier, count + 1)
    own = (0, 0, 0)
    for part in range(len(spread.parts)):
        spread.start_onward(part, own, spread.me)

    source = src_ref[...]
    rank = jnp.zeros_like(source)
    for place, (_, src) in enumerate(ranked):
        rank = rank + jnp.where(source == src, place, 0)
    block = source * per_src + off_ref[...]
    slot = slot_ref[...]
    pick = lambda v: [v[k : k + 1] for k in range(terms)]
    blocks, slots = sort_terms(pick(rank), (pick(block), pick(slot)))
    for k in range(terms):
        lists[k : k + 1, :] = blocks[k]
        lists[terms + k : terms + k + 1, :] = slots[k]
    to_index = pltpu.make_async_copy(lists, index, index_sem)
    to_index.start()

    local.wait()
    spread.run()
    to_index.wait()
    load_h.wait()

    def product(held, row, first, last):
        left = [held[index[k, row]] for k in range(first, last)]
        right = [h_ref[index[terms + k, row]] for k in range(first, last)]
        return jnp.dot(
            jnp.concatenate(left, axis=1),
            jnp.concatenate(right, axis=0),
            preferred_element_type=jnp.float32,
        )

    first, complete = 0, 0
    for width in STAGES[:-1]:
        last = first + width
        fresh = []
        for near, src in ranked[complete : cols - terms + last]:
            spread.wait_finals(near, src)
            where = pl.ds(src * per_src, per_src)
            copy = pltpu.make_async_copy(panel.at[where], ready.at[where], ready_sem.at[src])
            copy.start()
            fresh.append(copy)
        complete = cols - terms + last
        for copy in fresh:
            copy.wait()

        @pl.loop(0, rows, unroll=4)
        def _(row, first=first, last=last):
            value = product(ready, row, first, last)
            total[row] = value if first == 0 else total[row] + value

        first = last
    for near, src in ranked[complete:]:
        spread.wait_finals(near, src)

    def partial(row):
        value = product(panel, row, first, terms)
        return (total[row] + value if first else value).astype(jnp.bfloat16)

    size = keep // CHUNKS

    def swap(chunk):
        part = pl.ds(chunk * size, size)
        return pltpu.make_async_remote_copy(
            src_ref=theirs.at[part],
            dst_ref=arrived.at[part],
            send_sem=swap_send.at[chunk],
            recv_sem=swap_recv.at[chunk],
            device_id={"layer": 1 - layer},
            device_id_type=pl.DeviceIdType.MESH,
        )

    @pl.loop(0, CHUNKS)
    def _(chunk):
        @pl.loop(0, size, unroll=4)
        def _(i):
            p = chunk * size + i
            theirs[p] = partial((1 - layer) * keep + p)
        swap(chunk).start()

    @pl.loop(0, CHUNKS)
    def _(chunk):
        swap(chunk).wait_recv()

        @pl.loop(0, size, unroll=4)
        def _(i):
            p = chunk * size + i
            both = partial(layer * keep + p).astype(jnp.float32) + arrived[p].astype(jnp.float32)
            out_ref[p] = both.astype(out_ref.dtype)

    spread.finish()

    @pl.loop(0, CHUNKS)
    def _(chunk):
        swap(chunk).wait_send()


def on_device(cols, x_blocks, h_blocks, a_src, a_off, b_slot):
    x_local = x_blocks[0, 0]
    h = lax.all_gather(h_blocks[0, 0], "row", axis=0, tiled=True)
    per_src, bs = x_local.shape[0], x_local.shape[1]
    rows, terms = a_src.shape[3:]
    parts = len(shares(per_src))
    vmem = pl.BlockSpec(memory_space=pltpu.VMEM)
    hbm = pl.BlockSpec(memory_space=pltpu.HBM)
    panel = pltpu.VMEM((cols * per_src, bs, bs), jnp.bfloat16)
    half = pltpu.VMEM((rows // 2, bs, bs), jnp.bfloat16)
    out = pl.pallas_call(
        kernel,
        out_shape=jax.ShapeDtypeStruct((rows // 2, bs, bs), jnp.bfloat16),
        in_specs=[vmem, vmem, vmem, vmem, hbm],
        out_specs=vmem,
        scratch_shapes=[
            panel,
            panel,
            pltpu.VMEM((rows, bs, bs), jnp.float32),
            pltpu.VMEM(h.shape, jnp.bfloat16),
            half,
            half,
            pltpu.VMEM((2 * terms, rows), jnp.int32),
            pltpu.SMEM((2 * terms, rows), jnp.int32),
            pltpu.SemaphoreType.DMA,
            pltpu.SemaphoreType.DMA,
            pltpu.SemaphoreType.DMA,
            pltpu.SemaphoreType.DMA((cols,)),
            pltpu.SemaphoreType.DMA((parts, cols, 6)),
            pltpu.SemaphoreType.DMA((parts, cols)),
            pltpu.SemaphoreType.DMA((CHUNKS,)),
            pltpu.SemaphoreType.DMA((CHUNKS,)),
        ],
        compiler_params=pltpu.CompilerParams(
            collective_id=0, has_side_effects=True, vmem_limit_bytes=56 << 20
        ),
    )(a_src[0, 0, 0].T, a_off[0, 0, 0].T, b_slot[0, 0, 0].T, x_local, h)
    return out[None, None]


def solution(mesh):
    placed = P("row", "col", "layer", None, None)
    return jax.shard_map(
        functools.partial(on_device, mesh.shape["col"]),
        mesh=mesh,
        in_specs=(placed,) * 5,
        out_specs=placed,
        check_vma=False,
    )
```

time: 91.1 us -> 88.2 us (0.968)
  local copies, waits for them, and re-layouts: 5.08 us -> 3.16 us
    unnamed x7 -> x1, local copies, waits for them, and re-layouts: 4.97 us -> 3.16 us
where the time goes in v3:
time: 88.2 us; the launch traced here: 88 us
  Pallas kernels  84.8 us (96%)
  local copies, waits for them, and re-layouts  3.16 us (4%)
    pallas_call x1, Pallas kernels, on_device(): pl.pallas_call(kernel, out_shape=jax.ShapeDtypeStruct((rows // 2, bs, bs)...  84.8 us
    unnamed x1, local copies, waits for them, and re-layouts  3.16 us

profile of v3, /device:TPU:0, one launch (start us, length us, event | category | flops | bytes accessed | tf_op | source)
XLA Modules:
  0.0 88.0 jit_solution(6859049499861520122)
XLA Ops:
  0.0 84.8 %shard_map.55 = bf16[64,128,128]{2,1,0:T(8,128)(2,1)} custom-call(s32[8,128]{1,0:T(8,128)} %bitcast.15, s32[8,128]{1,0:T(8,128)} %bitcast.16, s32[8,128]{1,0:T(8,128)} %bitcast.17, bf16[16,128,128]{2,1,0:T(8,128)(2,1)} %bitcast.13, bf16[16,128,128]{2,1,0:T(8,128)(2,1)} %bitcast.14), custom_call_target="tpu_custom_call" | custom-call | tf_op jit(solution)/shard_map/pallas_call | solution.py:334
  84.8 3.2 %copy.7 = bf16[1,1,64,128,128]{4,3,2,1,0:T(8,128)(2,1)} copy(bf16[1,1,64,128,128]{4,3,2,1,0:T(8,128)(2,1)} %bitcast.12) | data formatting | bytes 4194304
